TPU v7x, 256 devices: a whole 4x4x8 slice. The times are simulated.
256 devices in a mesh: seq: 16 (over z_lo, x), layer: 16 (over z_hi, y, core).
Axes of the slice: x: 4, y: 4, z: 8 (z_hi: 2, z_lo: 4; z = z_hi * 4 + z_lo), core: 2. Of those that a mesh axis runs over, the one named last changes fastest.
Arguments:
- train_inputs: bfloat16 [16, 2048, 4096], P('layer', 'seq'), may hold values from -6 to 6
- out_grads: bfloat16 [16, 2048, 14336], P('layer', 'seq'), may hold values from -6 to 6
- query_blocks: bfloat16 [16, 14336, 4096], P('layer', 'seq'), may hold values from -0.00018310547 to 0.00018310547
- basis_in: bfloat16 [16, 32, 128, 128], P('layer'), may hold values from -0.5 to 0.5
- basis_out: bfloat16 [16, 112, 128, 128], P('layer', 'seq'), may hold values from -0.5 to 0.5
- block_of: int32 [16, 16], P('layer'), may hold values from 0 to 15, each once within a row
Outputs:
- scores: float32 [2048], P('seq')
Inputs may be any that keep to these rules, and one draw needn't show every extreme that they name: Each row of block_of names every eigenbasis block of its layer once.
All inputs are finite; a program needn't handle non-finite values.
Results may differ from a plain program's by a relative error of at most 0.0055.
Values may be sent and summed in bfloat16 or wider, within the bound.
A program may use at most 128 MiB of HBM per device.

v0:
```python
import jax
import jax.numpy as jnp
from jax import lax
from jax.sharding import PartitionSpec as P


def turn_rows(rows, basis):
    count = rows.shape[0]
    groups = rows.reshape(count, basis.shape[0], basis.shape[1])
    turned = jnp.einsum("tnr,nrs->tns", groups, basis, preferred_element_type=jnp.float32)
    return turned.reshape(count, -1).astype(jnp.bfloat16)


def body(train_inputs, out_grads, query_blocks, basis_in, basis_out, block_of):
    acts = train_inputs[0]
    grads = out_grads[0]
    query = query_blocks[0]
    owners = block_of[0]
    count = acts.shape[0]
    rotated = turn_rows(acts, basis_in[0])
    outgoing = jnp.take(grads.reshape(count, owners.shape[0], -1), owners, axis=1)
    arrived = lax.all_to_all(outgoing, "seq", split_axis=1, concat_axis=0, tiled=True)
    turned = turn_rows(arrived.reshape(arrived.shape[0], -1), basis_out[0])
    partial_scores = jnp.sum(
        lax.dot_general(
            lax.all_gather(rotated, "seq", axis=0, tiled=True),
            query,
            (((1,), (1,)), ((), ())),
            preferred_element_type=jnp.float32,
        )
        * turned.astype(jnp.float32),
        axis=1,
    )
    share = lax.psum_scatter(partial_scores, "seq", scatter_dimension=0, tiled=True)
    return lax.psum(share, "layer")


def solution(mesh):
    placed = (
        P("layer", "seq", None),
        P("layer", "seq", None),
        P("layer", "seq", None),
        P("layer", None, None, None),
        P("layer", "seq", None, None),
        P("layer", None),
    )
    return jax.shard_map(body, mesh=mesh, in_specs=placed, out_specs=P("seq"), check_vma=False)
```

profile of v0, /device:TPU:1, one launch (start us, length us, event | category | flops | bytes accessed | tf_op | source)
XLA Modules:
  0.0 403.0 jit_solution(5762240686603335657)
XLA Ops:
  6.5 0.0 copy-start
  6.5 0.0 all-gather.2.cloned.1.call-start
  6.5 1.5 copy.35
  8.1 0.0 copy-done
  8.1 1.9 convolution_convert_fusion
  10.0 0.0 all-gather.2.cloned.1.call-update
  10.0 6.1 %copy.24 = bf16[1,128,14336]{1,2,0:T(8,128)(2,1)} copy(bf16[1,128,14336]{2,1,0:T(8,128)(2,1)} %param.7) | data formatting | bytes 7340032 | tf_op args[1]
  16.0 0.0 copy-start.2
  16.0 6.1 %copy.25 = bf16[128,16,896]{2,0,1:T(8,128)(2,1)} copy(bf16[128,16,896]{0,2,1:T(8,128)(2,1)} %bitcast.41) | data formatting | bytes 7340032 | tf_op jit(solution)/shard_map/reshape;squeeze | solution.py:21
  22.2 0.0 copy-done.2
  22.2 4.8 %gather_fusion = bf16[16,128,896]{2,1,0:T(8,128)(2,1)} fusion(bf16[128,16,896]{2,0,1:T(8,128)(2,1)} %copy.25, s32[1024]{0:T(1024)S(1)} %pad_clamp_fusion), kind=kCustom, calls=%fused_computation | custom fusion | bytes 7340096 | tf_op jit(solution)/shard_map/jit(_take)/gather | solution.py:21
  27.0 4.4 %select_bitcast_fusion = bf16[128,16,896]{2,0,1:T(8,128)(2,1)} fusion(bf16[16,128,896]{2,1,0:T(8,128)(2,1)} %gather_fusion, pred[16]{0:T(512)(128)(4,1)S(1)} %compare_and_fusion), kind=kLoop, calls=%fused_computation.7 | loop fusion | flops 1835008 | bytes 7340048 | tf_op jit(solution)/shard_map/jit(_take)/select_n | solution.py:21
  31.4 9.2 %all-to-all-start = ((bf16[128,16,896]{2,0,1:T(8,128)(2,1)}), bf16[128,16,896]{2,0,1:T(8,128)(2,1)}, u32[]{:S(2)}, u32[]{:S(2)}) async-start(bf16[128,16,896]{2,0,1:T(8,128)(2,1)} %select_bitcast_fusion), calls=%async_computation | async-start | bytes 7340032 | tf_op jit(solution)/shard_map/all_to_all | solution.py:22
  40.6 0.0 copy-done.3
  40.6 0.6 dynamic-slice
  41.9 182.5 %all-to-all-done = bf16[128,16,896]{2,0,1:T(8,128)(2,1)} async-done(((bf16[128,16,896]{2,0,1:T(8,128)(2,1)}), bf16[128,16,896]{2,0,1:T(8,128)(2,1)}, u32[]{:S(2)}, u32[]{:S(2)}) %all-to-all-start) | async-done | bytes 3670048 | tf_op jit(solution)/shard_map/all_to_all | solution.py:22
  224.3 8.1 %reshape.50 = bf16[2048,7,128]{2,1,0:T(8,128)(2,1)} reshape(bf16[16,128,1,896]{3,1,0,2:T(8,128)(2,1)} %bitcast.10) | data formatting | bytes 7340032 | tf_op jit(solution)/shard_map/reshape;reshape | solution.py:9
  232.4 0.0 copy-done.1
  232.4 6.3 %convert_convert_fusion = f32[7,2048,128]{1,2,0:T(8,128)} fusion(bf16[2048,7,128]{2,1,0:T(8,128)(2,1)} %reshape.50, bf16[1,7,128,128]{3,2,1,0:T(8,128)(2,1)S(1)} %copy-done.1), kind=kOutput, calls=%fused_computation.8 | convolution fusion | flops 473432064 | bytes 11239424 | tf_op jit(solution)/shard_map/tnr,nrs->tns/dot_general | solution.py:10
  238.7 42.3 %all-gather.2.cloned.1.call-done = bf16[2048,4096]{0,1:T(8,128)(2,1)} async-done(((bf16[128,4096]{0,1:T(8,128)(2,1)}), bf16[2048,4096]{0,1:T(8,128)(2,1)}) %all-gather.2.cloned.1.call-update) | async-done | bytes 16777232 | tf_op jit(solution)/shard_map/all_gather | solution.py:26
  281.1 20.8 %fusion = f32[2048]{0:T(1024)S(1)} fusion(f32[7,2048,128]{1,2,0:T(8,128)} %convert_convert_fusion, bf16[2048,4096]{0,1:T(8,128)(2,1)} %all-gather.2.cloned.1.call-done, bf16[1,896,4096]{2,1,0:T(8,128)(2,1)} %param.8), kind=kOutput, calls=%fused_computation.2 | convolution fusion | flops 15036053504 | bytes 31465472 | tf_op jit(solution)/shard_map/dot_general | solution.py:25
  301.9 43.9 %all-reduce = f32[2048]{0:T(1024)S(1)} all-reduce(f32[2048]{0:T(1024)S(1)} %fusion), channel_id=2, replica_groups=mesh['seq'=16,'layer'=16] {'seq'}, use_global_device_ids=true, to_apply=%region_1.2.clone | all-reduce | flops 2048 | bytes 16384
  345.8 0.1 dynamic-slice.1
  345.9 50.3 %psum.7 = f32[128]{0:T(128)} all-reduce(f32[128]{0:T(128)S(1)} %dynamic-slice.1), channel_id=1, replica_groups=mesh['seq'=16,'layer'=16] {'layer'}, use_global_device_ids=true, to_apply=%region_2.3 | all-reduce | flops 128 | bytes 1024 | tf_op jit(solution)/shard_map/psum | solution.py:35
  (5 shorter events, 0.0 us)
Async XLA Ops:
  6.5 1.6 copy-start
  6.5 274.5 %all-gather.2.cloned.1.call-start = ((), (), s32[]{:S(2)}) async-start(), calls=%async_computation.1 | async-start | bytes 17825792 | tf_op jit(solution)/shard_map/all_gather | solution.py:26
  16.0 6.1 %copy-start.2 = (s32[1,16]{1,0:T(1,128)S(1)}, s32[1,16]{1,0:T(1,128)}, u32[]{:S(2)}) copy-start(s32[1,16]{1,0:T(1,128)} %param.11) | copy-start | bytes 196
  31.4 9.2 %copy-start.3 = (u32[256]{0:T(256)S(1)}, u32[256]{0:T(256)}, u32[]{:S(2)}) copy-start(u32[256]{0:T(256)} %constant.26) | copy-start | bytes 3076
  31.4 192.9 %all-to-all-start = ((bf16[128,16,896]{2,0,1:T(8,128)(2,1)}), bf16[128,16,896]{2,0,1:T(8,128)(2,1)}, u32[]{:S(2)}, u32[]{:S(2)}) async-start(bf16[128,16,896]{2,0,1:T(8,128)(2,1)} %select_bitcast_fusion), calls=%async_computation | async-start | bytes 7340032 | tf_op jit(solution)/shard_map/all_to_all | solution.py:22
  224.3 8.1 %copy-start.1 = (bf16[1,7,128,128]{3,2,1,0:T(8,128)(2,1)S(1)}, bf16[1,7,128,128]{3,2,1,0:T(8,128)(2,1)}, u32[]{:S(2)}) copy-start(bf16[1,7,128,128]{3,2,1,0:T(8,128)(2,1)} %param.10) | copy-start | bytes 688132
Sparse Core Ops, SparseCore 0:
  10.1 270.9 all-gather.1
where the time goes:
time: 404 us; the launch traced here: 403 us
  waiting for transfers between devices  225 us (56%)
  blocking collectives  94.2 us (23%)
  matrix products  29 us (7%)
  local copies, waits for them, and re-layouts  27.3 us (7%)
  between operations  14.1 us (3%)
  starting transfers between devices  9.22 us (2%)
  other arithmetic  4.39 us (1%)
    all_to_all x1, waiting for transfers between devices, body(): lax.all_to_all(outgoing, 'seq', split_axis=1, concat_axis=0, tiled=True)  182 us
    psum x1, blocking collectives, body(): return lax.psum(share, 'layer')  50.3 us
    unnamed x1, blocking collectives  43.9 us
    all_gather x1, waiting for transfers between devices, body(): lax.all_gather(rotated, 'seq', axis=0, tiled=True)  42.3 us
    dot_general x1, matrix products, body(): lax.dot_general(lax.all_gather(rotated, 'seq', axis=0, tiled=True), query...  20.8 us
    all_to_all x1, starting transfers between devices, body(): lax.all_to_all(outgoing, 'seq', split_axis=1, concat_axis=0, tiled=True)  9.22 us
    unnamed x12, local copies, waits for them, and re-layouts  8.29 us
    dot_general x2, matrix products, turn_rows(): jnp.einsum('tnr,nrs->tns', groups, basis, preferred_element_type=jnp.floa...  8.17 us
  transfers between devices with their start and end apart: 2, of which 2 were waited for; matrix products, arithmetic and copies ran while one was open for 9% of the time, Pallas kernels for 0%

commit v1 on v0

--- a/solution.py
+++ b/solution.py
@@ -1,7 +1,13 @@
+import functools
+
 import jax
 import jax.numpy as jnp
 from jax import lax
+from jax.experimental import pallas as pl
+from jax.experimental.pallas import tpu as pltpu
 from jax.sharding import PartitionSpec as P
+
+MESH = pl.DeviceIdType.MESH
 
 
 def turn_rows(rows, basis):
@@ -11,7 +17,82 @@
     return turned.reshape(count, -1).astype(jnp.bfloat16)
 
 
-def body(train_inputs, out_grads, query_blocks, basis_in, basis_out, block_of):
+def reduce_kernel(ns, nl, part_ref, out_ref, slots1, mine, slots2, ssem1, rsem1, ssem2, rsem2):
+    ms = lax.axis_index("seq")
+    ml = lax.axis_index("layer")
+    barrier = pltpu.get_barrier_semaphore()
+    for d in range(1, ns):
+        pl.semaphore_signal(barrier, inc=1, device_id=(lax.rem(ms + d, ns), ml), device_id_type=MESH)
+    for d in range(1, nl):
+        pl.semaphore_signal(barrier, inc=1, device_id=(ms, lax.rem(ml + d, nl)), device_id_type=MESH)
+    pl.semaphore_wait(barrier, (ns - 1) + (nl - 1))
+
+    sends = []
+    for d in range(1, ns):
+        j = lax.rem(ms + d, ns)
+        c = pltpu.make_async_remote_copy(
+            src_ref=part_ref.at[j], dst_ref=slots1.at[ms], send_sem=ssem1.at[j], recv_sem=rsem1.at[ms],
+            device_id=(j, ml), device_id_type=MESH)
+        c.start()
+        sends.append(c)
+    slots1[ms] = part_ref[ms]
+    for d in range(1, ns):
+        i = lax.rem(ms + ns - d, ns)
+        pltpu.make_async_remote_copy(
+            src_ref=part_ref.at[i], dst_ref=slots1.at[i], send_sem=ssem1.at[i], recv_sem=rsem1.at[i],
+            device_id=(i, ml), device_id_type=MESH).wait_recv()
+    for c in sends:
+        c.wait_send()
+    acc = slots1[0]
+    for i in range(1, ns):
+        acc = acc + slots1[i]
+    mine[...] = acc
+
+    sends = []
+    for d in range(1, nl):
+        j = lax.rem(ml + d, nl)
+        c = pltpu.make_async_remote_copy(
+            src_ref=mine, dst_ref=slots2.at[ml], send_sem=ssem2.at[j], recv_sem=rsem2.at[ml],
+            device_id=(ms, j), device_id_type=MESH)
+        c.start()
+        sends.append(c)
+    slots2[ml] = acc
+    for d in range(1, nl):
+        i = lax.rem(ml + nl - d, nl)
+        pltpu.make_async_remote_copy(
+            src_ref=mine, dst_ref=slots2.at[i], send_sem=ssem2.at[i], recv_sem=rsem2.at[i],
+            device_id=(ms, i), device_id_type=MESH).wait_recv()
+    for c in sends:
+        c.wait_send()
+    tot = slots2[0]
+    for i in range(1, nl):
+        tot = tot + slots2[i]
+    out_ref[...] = tot
+
+
+def reduce_scores(partial, ns, nl):
+    w = partial.shape[0] // ns
+    part = partial.reshape(ns, 1, w)
+    out = pl.pallas_call(
+        functools.partial(reduce_kernel, ns, nl),
+        out_shape=jax.ShapeDtypeStruct((1, w), jnp.float32),
+        in_specs=[pl.BlockSpec(memory_space=pltpu.VMEM)],
+        out_specs=pl.BlockSpec(memory_space=pltpu.VMEM),
+        scratch_shapes=[
+            pltpu.VMEM((ns, 1, w), jnp.float32),
+            pltpu.VMEM((1, w), jnp.float32),
+            pltpu.VMEM((nl, 1, w), jnp.float32),
+            pltpu.SemaphoreType.DMA((ns,)),
+            pltpu.SemaphoreType.DMA((ns,)),
+            pltpu.SemaphoreType.DMA((nl,)),
+            pltpu.SemaphoreType.DMA((nl,)),
+        ],
+        compiler_params=pltpu.CompilerParams(collective_id=0, has_side_effects=True),
+    )(part)
+    return out.reshape(w)
+
+
+def body(ns, nl, train_inputs, out_grads, query_blocks, basis_in, basis_out, block_of):
     acts = train_inputs[0]
     grads = out_grads[0]
     query = query_blocks[0]
@@ -31,11 +112,11 @@
         * turned.astype(jnp.float32),
         axis=1,
     )
-    share = lax.psum_scatter(partial_scores, "seq", scatter_dimension=0, tiled=True)
-    return lax.psum(share, "layer")
+    return reduce_scores(partial_scores, ns, nl)
 
 
 def solution(mesh):
+    ns, nl = mesh.shape["seq"], mesh.shape["layer"]
     placed = (
         P("layer", "seq", None),
         P("layer", "seq", None),
@@ -44,4 +125,4 @@
         P("layer", "seq", None, None),
         P("layer", None),
     )
-    return jax.shard_map(body, mesh=mesh, in_specs=placed, out_specs=P("seq"), check_vma=False)
+    return jax.shard_map(functools.partial(body, ns, nl), mesh=mesh, in_specs=placed, out_specs=P("seq"), check_vma=False)

time: 404 us -> 340 us (0.84)
  waiting for transfers between devices: 225 us -> 21.6 us
  blocking collectives: 94.2 us -> 214 us
  Pallas kernels: 0 us -> 30.3 us
  starting transfers between devices: 9.22 us -> 0.01 us
    all_to_all x0 -> x1, blocking collectives: none -> 214 us  [body(): lax.all_to_all(outgoing, 'seq', split_axis=1, concat_axis=0, tiled=True)]
    all_to_all x1 -> x0, waiting for transfers between devices: 182 us -> none  [body(): lax.all_to_all(outgoing, 'seq', split_axis=1, concat_axis=0, tiled=True)]
    psum x1 -> x0, blocking collectives: 50.3 us -> none  [body(): return lax.psum(share, 'layer')]
    unnamed x1 -> x0, blocking collectives: 43.9 us -> none
    pallas_call x0 -> x1, Pallas kernels: none -> 30.3 us  [reduce_scores(): pl.pallas_call(functools.partial(reduce_kernel, ns, nl), out_shape=jax.Sh...]
    all_gather x1, waiting for transfers between devices: 42.3 us -> 21.6 us  [body(): lax.all_gather(rotated, 'seq', axis=0, tiled=True)]
    all_to_all x1 -> x0, starting transfers between devices: 9.22 us -> none  [body(): lax.all_to_all(outgoing, 'seq', split_axis=1, concat_axis=0, tiled=True)]
    unnamed x12 -> x9, local copies, waits for them, and re-layouts: 8.29 us -> 8.76 us
  transfers between devices with their start and end apart: 2 -> 1, of which waited for: 2 -> 1; matrix products, arithmetic and copies ran while one was open for 9% -> 10% of each run, Pallas kernels for 0% -> 0%
where the time goes in v1:
time: 340 us
  blocking collectives  214 us (63%)
  Pallas kernels  30.3 us (9%)
  matrix products  29.6 us (9%)
  local copies, waits for them, and re-layouts  27.8 us (8%)
  waiting for transfers between devices  21.6 us (6%)
  between operations  13.4 us (4%)
    all_to_all x1, blocking collectives, body(): lax.all_to_all(outgoing, 'seq', split_axis=1, concat_axis=0, tiled=True)  214 us
    pallas_call x1, Pallas kernels, reduce_scores(): pl.pallas_call(functools.partial(reduce_kernel, ns, nl), out_shape=jax.Sh...  30.3 us
    all_gather x1, waiting for transfers between devices, body(): lax.all_gather(rotated, 'seq', axis=0, tiled=True)  21.6 us
    dot_general x1, matrix products, body(): lax.dot_general(lax.all_gather(rotated, 'seq', axis=0, tiled=True), query...  21.4 us
    unnamed x9, local copies, waits for them, and re-layouts  8.76 us
    dot_general x2, matrix products, turn_rows(): jnp.einsum('tnr,nrs->tns', groups, basis, preferred_element_type=jnp.floa...  8.2 us
    another operation x1, local copies, waits for them, and re-layouts, turn_rows(): groups = rows.reshape(count, basis.shape[0], basis.shape[1])  8.09 us
  transfers between devices with their start and end apart: 1, of which 1 were waited for; matrix products, arithmetic and copies ran while one was open for 10% of the time, Pallas kernels for 0%

profile of v1, /device:TPU:1, one launch (start us, length us, event | category | flops | bytes accessed | tf_op | source)
XLA Modules:
  0.0 339.7 jit_solution(10377578156614264684)
XLA Ops:
  6.5 0.0 copy-start
  6.5 0.0 all-gather.2.cloned.1.call-start
  6.5 1.5 copy.28
  8.1 0.0 copy-done
  8.1 1.9 convolution_convert_fusion
  10.0 0.0 all-gather.2.cloned.1.call-update
  10.0 6.1 %copy.17 = bf16[1,128,14336]{1,2,0:T(8,128)(2,1)} copy(bf16[1,128,14336]{2,1,0:T(8,128)(2,1)} %param.7) | data formatting | bytes 7340032 | tf_op args[1]
  16.0 0.0 copy-start.2
  16.0 6.1 %copy.18 = bf16[128,16,896]{2,0,1:T(8,128)(2,1)} copy(bf16[128,16,896]{0,2,1:T(8,128)(2,1)} %bitcast.42) | data formatting | bytes 7340032 | tf_op jit(solution)/shard_map/reshape;squeeze | solution.py:102
  22.1 0.0 copy-done.2
  22.1 4.8 %gather_fusion = bf16[16,128,896]{2,1,0:T(8,128)(2,1)} fusion(bf16[128,16,896]{2,0,1:T(8,128)(2,1)} %copy.18, s32[1024]{0:T(1024)S(1)} %pad_clamp_fusion), kind=kCustom, calls=%fused_computation | custom fusion | bytes 7340096 | tf_op jit(solution)/shard_map/jit(_take)/gather | solution.py:102
  27.0 2.5 select_bitcast_fusion
  29.5 214.4 %all_to_all.15 = bf16[128,16,896]{2,0,1:T(8,128)(2,1)} all-to-all(bf16[128,16,896]{2,0,1:T(8,128)(2,1)S(1)} %select_bitcast_fusion), channel_id=1, replica_groups=mesh['seq'=16,'layer'=16] {'seq'}, dimensions={1} | all-to-all | bytes 7340032 | tf_op jit(solution)/shard_map/all_to_all | solution.py:103
  243.9 0.0 copy-start.1
  243.9 8.1 %reshape.58 = bf16[2048,7,128]{2,1,0:T(8,128)(2,1)} reshape(bf16[16,128,1,896]{3,1,0,2:T(8,128)(2,1)} %bitcast.43) | data formatting | bytes 7340032 | tf_op jit(solution)/shard_map/reshape;reshape | solution.py:15
  252.0 0.0 copy-done.1
  252.0 6.3 %convert_convert_fusion = f32[7,2048,128]{1,2,0:T(8,128)} fusion(bf16[2048,7,128]{2,1,0:T(8,128)(2,1)} %reshape.58, bf16[1,7,128,128]{3,2,1,0:T(8,128)(2,1)S(1)} %copy-done.1), kind=kOutput, calls=%fused_computation.8 | convolution fusion | flops 473432064 | bytes 11239424 | tf_op jit(solution)/shard_map/tnr,nrs->tns/dot_general | solution.py:16
  258.3 21.6 %all-gather.2.cloned.1.call-done = bf16[2048,4096]{0,1:T(8,128)(2,1)} async-done(((bf16[128,4096]{0,1:T(8,128)(2,1)}), bf16[2048,4096]{0,1:T(8,128)(2,1)}) %all-gather.2.cloned.1.call-update) | async-done | bytes 16777232 | tf_op jit(solution)/shard_map/all_gather | solution.py:107
  279.9 21.4 %fusion = f32[2048]{0:T(1024)} fusion(f32[7,2048,128]{1,2,0:T(8,128)} %convert_convert_fusion, bf16[2048,4096]{0,1:T(8,128)(2,1)} %all-gather.2.cloned.1.call-done, bf16[1,896,4096]{2,1,0:T(8,128)(2,1)} %param.8), kind=kOutput, calls=%fused_computation.2 | convolution fusion | flops 15036053504 | bytes 31465472 | tf_op jit(solution)/shard_map/dot_general | solution.py:106
  301.3 30.3 %shard_map.64 = f32[1,128]{1,0:T(1,128)} custom-call(f32[16,1,128]{2,1,0:T(1,128)} %bitcast.47), custom_call_target="tpu_custom_call" | custom-call | tf_op jit(solution)/shard_map/pallas_call | solution.py:76
  331.7 1.1 copy.36
  (3 shorter events, 0.0 us)
Async XLA Ops:
  6.5 1.6 copy-start
  6.5 273.4 %all-gather.2.cloned.1.call-start = ((), (), s32[]{:S(2)}) async-start(), calls=%async_computation.1 | async-start | bytes 17825792 | tf_op jit(solution)/shard_map/all_gather | solution.py:107
  16.0 6.1 %copy-start.2 = (s32[1,16]{1,0:T(1,128)S(1)}, s32[1,16]{1,0:T(1,128)}, u32[]{:S(2)}) copy-start(s32[1,16]{1,0:T(1,128)} %param.11) | copy-start | bytes 196
  243.9 8.1 %copy-start.1 = (bf16[1,7,128,128]{3,2,1,0:T(8,128)(2,1)S(1)}, bf16[1,7,128,128]{3,2,1,0:T(8,128)(2,1)}, u32[]{:S(2)}) copy-start(bf16[1,7,128,128]{3,2,1,0:T(8,128)(2,1)} %param.10) | copy-start | bytes 688132
Sparse Core Ops, SparseCore 0:
  10.1 269.7 all-gather.1

commit v2 on v1

--- a/solution.py
+++ b/solution.py
@@ -68,6 +68,108 @@
     for i in range(1, nl):
         tot = tot + slots2[i]
     out_ref[...] = tot
+
+
+def comm_kernel(nx, nz, r1, x_ref, g_ref, xo_ref, go_ref, ssem, rsem, gssem, grsem, lsem):
+    ns = nx * nz
+    t = x_ref.shape[0]
+    s = lax.axis_index("seq")
+    lay = lax.axis_index("layer")
+    zl = s // nx
+    xx = lax.rem(s, nx)
+    parts = (pl.ds(0, r1), pl.ds(r1, t - r1))
+
+    def at(dz, dx):
+        return lax.rem(zl + dz, nz) * nx + lax.rem(xx + dx, nx)
+
+    barrier = pltpu.get_barrier_semaphore()
+    for d in range(1, ns):
+        pl.semaphore_signal(barrier, inc=1, device_id=(lax.rem(s + d, ns), lay), device_id_type=MESH)
+    pl.semaphore_wait(barrier, ns - 1)
+
+    own_x = pltpu.make_async_copy(x_ref, xo_ref.at[s], lsem.at[0])
+    own_g = pltpu.make_async_copy(g_ref.at[s], go_ref.at[s], lsem.at[1])
+    own_x.start()
+    own_g.start()
+
+    sends = []
+
+    def send(src, slot, part, dst):
+        c = pltpu.make_async_remote_copy(
+            src_ref=src, dst_ref=xo_ref.at[slot, parts[part]], send_sem=ssem.at[len(sends)],
+            recv_sem=rsem.at[slot * 2 + part], device_id=(dst, lay), device_id_type=MESH)
+        c.start()
+        sends.append(c)
+
+    def recv(slot, part):
+        pltpu.make_async_remote_copy(
+            src_ref=x_ref.at[parts[part]], dst_ref=xo_ref.at[slot, parts[part]], send_sem=ssem.at[0],
+            recv_sem=rsem.at[slot * 2 + part], device_id=(slot, lay), device_id_type=MESH).wait_recv()
+
+    for dx in range(1, nx):
+        send(x_ref.at[parts[0]], s, 0, at(0, dx))
+    for dz in range(1, nz):
+        send(x_ref.at[parts[1]], s, 1, at(dz, 0))
+    for dz in range(1, nz):
+        send(x_ref.at[parts[0]], s, 0, at(dz, 0))
+    for dx in range(1, nx):
+        send(x_ref.at[parts[1]], s, 1, at(0, dx))
+    gsends = []
+    for d in range(1, ns):
+        j = lax.rem(s + d, ns)
+        c = pltpu.make_async_remote_copy(
+            src_ref=g_ref.at[j], dst_ref=go_ref.at[s], send_sem=gssem.at[d - 1],
+            recv_sem=grsem.at[s], device_id=(j, lay), device_id_type=MESH)
+        c.start()
+        gsends.append(c)
+    for dx in range(1, nx):
+        q = at(0, dx)
+        recv(q, 0)
+        for dz in range(1, nz):
+            send(xo_ref.at[q, parts[0]], q, 0, at(dz, 0))
+    for dz in range(1, nz):
+        q = at(dz, 0)
+        recv(q, 1)
+        for dx in range(1, nx):
+            send(xo_ref.at[q, parts[1]], q, 1, at(0, dx))
+    for dz in range(1, nz):
+        for dx in range(nx):
+            recv(at(dz, dx), 0)
+    for dx in range(1, nx):
+        for dz in range(nz):
+            recv(at(dz, dx), 1)
+    for d in range(1, ns):
+        i = lax.rem(s + ns - d, ns)
+        pltpu.make_async_remote_copy(
+            src_ref=g_ref.at[i], dst_ref=go_ref.at[i], send_sem=gssem.at[d - 1],
+            recv_sem=grsem.at[i], device_id=(i, lay), device_id_type=MESH).wait_recv()
+    for c in sends + gsends:
+        c.wait_send()
+    own_x.wait()
+    own_g.wait()
+
+
+def exchange(rotated, outgoing, ns):
+    nx = 4 if ns % 4 == 0 else 1
+    nz = ns // nx
+    t, dim = rotated.shape
+    w = outgoing.shape[-1]
+    r1 = (t * 3 // 8) // 16 * 16
+    n_sends = 2 * ((nx - 1) + (nz - 1)) + (nx - 1) * (nz - 1) * 2
+    return pl.pallas_call(
+        functools.partial(comm_kernel, nx, nz, r1),
+        out_shape=(jax.ShapeDtypeStruct((ns, t, dim), rotated.dtype), jax.ShapeDtypeStruct((ns, t, w), outgoing.dtype)),
+        in_specs=[pl.BlockSpec(memory_space=pl.ANY)] * 2,
+        out_specs=(pl.BlockSpec(memory_space=pl.ANY), pl.BlockSpec(memory_space=pl.ANY)),
+        scratch_shapes=[
+            pltpu.SemaphoreType.DMA((n_sends,)),
+            pltpu.SemaphoreType.DMA((2 * ns,)),
+            pltpu.SemaphoreType.DMA((ns - 1,)),
+            pltpu.SemaphoreType.DMA((ns,)),
+            pltpu.SemaphoreType.DMA((2,)),
+        ],
+        compiler_params=pltpu.CompilerParams(collective_id=1, has_side_effects=True),
+    )(rotated, outgoing)
 
 
 def reduce_scores(partial, ns, nl):
@@ -99,12 +201,12 @@
     owners = block_of[0]
     count = acts.shape[0]
     rotated = turn_rows(acts, basis_in[0])
-    outgoing = jnp.take(grads.reshape(count, owners.shape[0], -1), owners, axis=1)
-    arrived = lax.all_to_all(outgoing, "seq", split_axis=1, concat_axis=0, tiled=True)
-    turned = turn_rows(arrived.reshape(arrived.shape[0], -1), basis_out[0])
+    outgoing = jnp.take(grads.reshape(count, owners.shape[0], -1), owners, axis=1).transpose(1, 0, 2)
+    gathered, arrived = exchange(rotated, outgoing, ns)
+    turned = turn_rows(arrived.reshape(ns * count, -1), basis_out[0])
     partial_scores = jnp.sum(
         lax.dot_general(
-            lax.all_gather(rotated, "seq", axis=0, tiled=True),
+            gathered.reshape(ns * count, -1),
             query,
             (((1,), (1,)), ((), ())),
             preferred_element_type=jnp.float32,

time: 340 us -> 366 us (1.076)
  Pallas kernels: 30.3 us -> 305 us
  blocking collectives: 214 us -> 0 us
  waiting for transfers between devices: 21.6 us -> 0 us
  between operations: 13.4 us -> 0.06 us
  matrix products: 29.6 us -> 25.5 us
    pallas_call x0 -> x1, Pallas kernels: none -> 273 us  [exchange(): pl.pallas_call(functools.partial(comm_kernel, nx, nz, r1), out_shape=(jax...]
    all_to_all x1 -> x0, blocking collectives: 214 us -> none  [body(): lax.all_to_all(outgoing, 'seq', split_axis=1, concat_axis=0, tiled=True)]
    all_gather x1 -> x0, waiting for transfers between devices: 21.6 us -> none  [body(): lax.all_gather(rotated, 'seq', axis=0, tiled=True)]
    dot_general x2, matrix products: 8.2 us -> 4.22 us  [turn_rows(): jnp.einsum('tnr,nrs->tns', groups, basis, preferred_element_type=jnp.floa...]
    unnamed x9 -> x7, local copies, waits for them, and re-layouts: 8.76 us -> 8.66 us
  transfers between devices with their start and end apart: 1 -> 0, of which waited for: 1 -> 0; matrix products, arithmetic and copies ran while one was open for 10% -> 0% of each run, Pallas kernels for 0% -> 0%
where the time goes in v2:
time: 366 us; the launch traced here: 365 us
  Pallas kernels  305 us (83%)
  local copies, waits for them, and re-layouts  29.1 us (8%)
  matrix products  25.5 us (7%)
  other arithmetic  5.67 us (2%)
    pallas_call x1, Pallas kernels, exchange(): pl.pallas_call(functools.partial(comm_kernel, nx, nz, r1), out_shape=(jax...  273 us
    pallas_call x1, Pallas kernels, reduce_scores(): pl.pallas_call(functools.partial(reduce_kernel, ns, nl), out_shape=jax.Sh...  31.7 us
    dot_general x1, matrix products, body(): lax.dot_general(gathered.reshape(ns * count, -1), query, (((1,), (1,)), (...  21.3 us
    unnamed x7, local copies, waits for them, and re-layouts  8.66 us
    another operation x1, local copies, waits for them, and re-layouts, turn_rows(): groups = rows.reshape(count, basis.shape[0], basis.shape[1])  8.08 us

profile of v2, /device:TPU:1, one launch (start us, length us, event | category | flops | bytes accessed | tf_op | source)
XLA Modules:
  0.0 365.1 jit_solution(9234412139374114536)
XLA Ops:
  0.0 0.0 copy-start
  0.0 0.7 fusion.12
  0.8 0.7 compare_and_fusion
  1.4 1.5 copy.33
  2.9 0.0 copy-done
  2.9 0.9 convolution_convert_fusion
  3.8 1.4 copy.29.x_ref
  5.2 6.1 %copy.21 = bf16[1,128,14336]{1,2,0:T(8,128)(2,1)} copy(bf16[1,128,14336]{2,1,0:T(8,128)(2,1)} %param.7) | data formatting | bytes 7340032 | tf_op args[1]
  11.3 6.1 %copy.22 = bf16[128,16,896]{2,0,1:T(8,128)(2,1)} copy(bf16[128,16,896]{0,2,1:T(8,128)(2,1)} %bitcast.34) | data formatting | bytes 7340032 | tf_op jit(solution)/shard_map/reshape;squeeze | solution.py:204
  17.4 4.8 %gather_fusion = bf16[16,128,896]{2,1,0:T(8,128)(2,1)} fusion(bf16[128,16,896]{2,0,1:T(8,128)(2,1)} %copy.22, s32[1024]{0:T(1024)S(1)} %pad_clamp_fusion), kind=kCustom, calls=%fused_computation | custom fusion | bytes 7340096 | tf_op jit(solution)/shard_map/jit(_take)/gather | solution.py:204
  22.2 4.3 %broadcast_select_fusion.g_ref = bf16[16,128,896]{2,1,0:T(8,128)(2,1)} fusion(bf16[16,128,896]{2,1,0:T(8,128)(2,1)} %gather_fusion, pred[16]{0:T(512)(128)(4,1)S(1)} %compare_and_fusion), kind=kLoop, calls=%fused_computation.8 | loop fusion | flops 1835008 | bytes 7340048 | tf_op jit(solution)/shard_map/jit(_take)/select_n | solution.py:204
  26.5 273.1 %shard_map.64 = (bf16[16,128,4096]{2,1,0:T(8,128)(2,1)}, bf16[16,128,896]{2,1,0:T(8,128)(2,1)}) custom-call(bf16[128,4096]{1,0:T(8,128)(2,1)} %copy.29.x_ref, bf16[16,128,896]{2,1,0:T(8,128)(2,1)} %broadcast_select_fusion.g_ref), custom_call_target="tpu_custom_call" | custom-call | tf_op jit(solution)/shard_map/pallas_call | solution.py:159
  299.6 0.0 copy-start.1
  299.6 8.1 %reshape.61 = bf16[2048,7,128]{2,1,0:T(8,128)(2,1)} reshape(bf16[16,128,896]{2,1,0:T(8,128)(2,1)} %get-tuple-element.8) | data formatting | bytes 7340032 | tf_op jit(solution)/shard_map/reshape;reshape | solution.py:15
  307.7 0.0 copy-done.1
  307.7 3.3 convert_convert_fusion
  311.0 21.3 %fusion = f32[2048]{0:T(1024)} fusion(f32[7,2048,128]{1,2,0:T(8,128)S(1)} %convert_convert_fusion, bf16[2048,4096]{1,0:T(8,128)(2,1)} %bitcast.40, bf16[1,896,4096]{2,1,0:T(8,128)(2,1)} %param.8), kind=kOutput, calls=%fused_computation.2 | convolution fusion | flops 15036053504 | bytes 31465472 | tf_op jit(solution)/shard_map/dot_general | solution.py:208
  332.3 31.7 %shard_map.65 = f32[1,128]{1,0:T(1,128)} custom-call(f32[16,1,128]{2,1,0:T(1,128)} %bitcast.38), custom_call_target="tpu_custom_call" | custom-call | tf_op jit(solution)/shard_map/pallas_call | solution.py:178
  364.0 1.1 copy.41
  (1 shorter events, 0.0 us)
Async XLA Ops:
  0.0 2.9 copy-start
  299.6 8.1 %copy-start.1 = (bf16[1,7,128,128]{3,2,1,0:T(8,128)(2,1)S(1)}, bf16[1,7,128,128]{3,2,1,0:T(8,128)(2,1)}, u32[]{:S(2)}) copy-start(bf16[1,7,128,128]{3,2,1,0:T(8,128)(2,1)} %param.10) | copy-start | bytes 688132

commit v3 on v2

--- a/solution.py
+++ b/solution.py
@@ -201,9 +201,14 @@
     owners = block_of[0]
     count = acts.shape[0]
     rotated = turn_rows(acts, basis_in[0])
-    outgoing = jnp.take(grads.reshape(count, owners.shape[0], -1), owners, axis=1).transpose(1, 0, 2)
+    width = grads.shape[1] // owners.shape[0]
+    outgoing = jnp.stack([lax.dynamic_slice_in_dim(grads, owners[k] * width, width, axis=1) for k in range(owners.shape[0])])
     gathered, arrived = exchange(rotated, outgoing, ns)
-    turned = turn_rows(arrived.reshape(ns * count, -1), basis_out[0])
+    arrived = arrived.reshape(ns * count, width)
+    rb = basis_out.shape[-1]
+    turned = jnp.concatenate(
+        [jnp.dot(arrived[:, e * rb:(e + 1) * rb], basis_out[0, e], preferred_element_type=jnp.float32) for e in range(basis_out.shape[1])],
+        axis=1).astype(jnp.bfloat16)
     partial_scores = jnp.sum(
         lax.dot_general(
             gathered.reshape(ns * count, -1),

time: 366 us -> 373 us (1.019)
  between operations: 0.06 us -> 10.2 us
  matrix products: 25.5 us -> 31.5 us
  other arithmetic: 5.67 us -> 0 us
  local copies, waits for them, and re-layouts: 29.1 us -> 25.1 us
    another operation x2 -> x1, local copies, waits for them, and re-layouts: 14.2 us -> 0.71 us  [body(): jnp.stack([lax.dynamic_slice_in_dim(grads, owners[k] * width, width, axis...]
    unnamed x7 -> x23, local copies, waits for them, and re-layouts: 8.66 us -> 21 us
    dot_general x0 -> x7, matrix products: none -> 9.67 us  [body(): jnp.dot(arrived[:, e * rb:(e + 1) * rb], basis_out[0, e], preferred_eleme...]
    select_n x2 -> x0, other arithmetic: 5 us -> none  [body(): jnp.take(grads.reshape(count, owners.shape[0], -1), owners, axis=1)]
    gather x1 -> x0, local copies, waits for them, and re-layouts: 4.79 us -> none  [body(): jnp.take(grads.reshape(count, owners.shape[0], -1), owners, axis=1)]
where the time goes in v3:
time: 373 us; the launch traced here: 372 us
  Pallas kernels  305 us (82%)
  matrix products  31.5 us (8%)
  local copies, waits for them, and re-layouts  25.1 us (7%)
  between operations  10.2 us (3%)
    pallas_call x1, Pallas kernels, exchange(): pl.pallas_call(functools.partial(comm_kernel, nx, nz, r1), out_shape=(jax...  273 us
    pallas_call x1, Pallas kernels, reduce_scores(): pl.pallas_call(functools.partial(reduce_kernel, ns, nl), out_shape=jax.Sh...  31.9 us
    unnamed x23, local copies, waits for them, and re-layouts  21 us
    dot_general x1, matrix products, body(): lax.dot_general(gathered.reshape(ns * count, -1), query, (((1,), (1,)), (...  21 us
    dot_general x7, matrix products, body(): jnp.dot(arrived[:, e * rb:(e + 1) * rb], basis_out[0, e], preferred_eleme...  9.67 us

profile of v3, /device:TPU:1, one launch (start us, length us, event | category | flops | bytes accessed | tf_op | source)
XLA Modules:
  0.0 371.8 jit_solution(2544744645780677012)
XLA Ops:
  0.0 1.9 fusion.34
  12.0 1.5 copy.12
  13.5 0.9 convolution_convert_fusion.7
  14.3 1.4 copy.11.x_ref
  15.7 1.8 dynamic-slice_dynamic-update-slice_fusion.15
  17.5 1.7 dynamic-slice_dynamic-update-slice_fusion.14
  19.2 1.6 dynamic-slice_dynamic-update-slice_fusion.13
  20.8 1.6 dynamic-slice_dynamic-update-slice_fusion.12
  22.4 1.7 dynamic-slice_dynamic-update-slice_fusion.11
  24.1 1.7 dynamic-slice_dynamic-update-slice_fusion.10
  25.8 1.7 dynamic-slice_dynamic-update-slice_fusion.9
  27.5 1.6 dynamic-slice_dynamic-update-slice_fusion.8
  29.1 0.7 dynamic-slice_dynamic-update-slice_fusion.7
  34.8 273.1 %shard_map.64 = (bf16[16,128,4096]{2,1,0:T(8,128)(2,1)}, bf16[16,128,896]{2,1,0:T(8,128)(2,1)}) custom-call(bf16[128,4096]{1,0:T(8,128)(2,1)} %copy.11.x_ref, bf16[16,128,896]{2,1,0:T(8,128)(2,1)} %dynamic-slice_dynamic-update-slice_fusion.g_ref), custom_call_target="tpu_custom_call" | custom-call | tf_op jit(solution)/shard_map/pallas_call | solution.py:159
  308.0 1.4 fusion.10
  309.4 1.4 fusion.9
  310.8 1.4 fusion.8
  312.2 1.4 fusion.7
  313.5 1.4 fusion.6
  314.9 1.4 fusion.5
  316.3 1.4 fusion.4
  317.7 21.0 %multiply_reduce_fusion = f32[2048]{0:T(1024)} fusion(bf16[2048,896]{0,1:T(8,128)(2,1)S(1)} %fusion.4, bf16[2048,4096]{1,0:T(8,128)(2,1)} %bitcast.68, bf16[1,896,4096]{2,1,0:T(8,128)(2,1)} %param.8), kind=kOutput, calls=%fused_computation.2 | convolution fusion | flops 15037888512 | bytes 27795456 | tf_op jit(solution)/shard_map/dot_general | solution.py:213
  338.7 31.9 %shard_map.65 = f32[1,128]{1,0:T(1,128)} custom-call(f32[16,1,128]{2,1,0:T(1,128)} %bitcast.66), custom_call_target="tpu_custom_call" | custom-call | tf_op jit(solution)/shard_map/pallas_call | solution.py:178
  370.6 1.2 copy.37
  (13 shorter events, 5.0 us)
Async XLA Ops:
  0.0 13.4 %copy-start = (bf16[1,32,128,128]{3,2,1,0:T(8,128)(2,1)S(1)}, bf16[1,32,128,128]{3,2,1,0:T(8,128)(2,1)}, u32[]{:S(2)}) copy-start(bf16[1,32,128,128]{3,2,1,0:T(8,128)(2,1)} %param.9) | copy-start | bytes 3145732
  15.7 13.4 %copy-start.1 = (bf16[1,128,14336]{2,1,0:T(8,128)(2,1)S(1)}, bf16[1,128,14336]{2,1,0:T(8,128)(2,1)}, u32[]{:S(2)}) copy-start(bf16[1,128,14336]{2,1,0:T(8,128)(2,1)} %param.7) | copy-start | bytes 11010052
  30.6 277.4 %copy-start.2 = (bf16[1,7,128,128]{3,2,1,0:T(8,128)(2,1)S(1)}, bf16[1,7,128,128]{3,2,1,0:T(8,128)(2,1)}, u32[]{:S(2)}) copy-start(bf16[1,7,128,128]{3,2,1,0:T(8,128)(2,1)} %param.10) | copy-start | bytes 688132

commit v4 on v3

--- a/solution.py
+++ b/solution.py
@@ -77,10 +77,12 @@
     lay = lax.axis_index("layer")
     zl = s // nx
     xx = lax.rem(s, nx)
-    parts = (pl.ds(0, r1), pl.ds(r1, t - r1))
+    ha, hb = r1 // 2, (t - r1) // 2
+    halves = ((pl.ds(0, ha), pl.ds(ha, ha)), (pl.ds(r1, hb), pl.ds(r1 + hb, hb)))
+    whole = (pl.ds(0, r1), pl.ds(r1, t - r1))
 
     def at(dz, dx):
-        return lax.rem(zl + dz, nz) * nx + lax.rem(xx + dx, nx)
+        return lax.rem(zl + dz + nz, nz) * nx + lax.rem(xx + dx + nx, nx)
 
     barrier = pltpu.get_barrier_semaphore()
     for d in range(1, ns):
@@ -94,26 +96,40 @@
 
     sends = []
 
-    def send(src, slot, part, dst):
-        c = pltpu.make_async_remote_copy(
-            src_ref=src, dst_ref=xo_ref.at[slot, parts[part]], send_sem=ssem.at[len(sends)],
-            recv_sem=rsem.at[slot * 2 + part], device_id=(dst, lay), device_id_type=MESH)
+    def rows(part, half):
+        return whole[part] if half is None else halves[part][half]
+
+    def sem(slot, part, half):
+        return rsem.at[slot * 4 + part * 2 + (0 if half is None else half)]
+
+    def send(dz, dx, part, half, to):
+        slot = at(dz, dx)
+        rr = rows(part, half)
+        src = x_ref.at[rr] if (dz, dx) == (0, 0) else xo_ref.at[slot, rr]
+        c = pltpu.make_async_remote_copy(
+            src_ref=src, dst_ref=xo_ref.at[slot, rr], send_sem=ssem.at[len(sends)],
+            recv_sem=sem(slot, part, half), device_id=(to, lay), device_id_type=MESH)
         c.start()
         sends.append(c)
 
-    def recv(slot, part):
-        pltpu.make_async_remote_copy(
-            src_ref=x_ref.at[parts[part]], dst_ref=xo_ref.at[slot, parts[part]], send_sem=ssem.at[0],
-            recv_sem=rsem.at[slot * 2 + part], device_id=(slot, lay), device_id_type=MESH).wait_recv()
-
-    for dx in range(1, nx):
-        send(x_ref.at[parts[0]], s, 0, at(0, dx))
-    for dz in range(1, nz):
-        send(x_ref.at[parts[1]], s, 1, at(dz, 0))
-    for dz in range(1, nz):
-        send(x_ref.at[parts[0]], s, 0, at(dz, 0))
-    for dx in range(1, nx):
-        send(x_ref.at[parts[1]], s, 1, at(0, dx))
+    def recv(dz, dx, part, half):
+        slot = at(dz, dx)
+        rr = rows(part, half)
+        pltpu.make_async_remote_copy(
+            src_ref=x_ref.at[rr], dst_ref=xo_ref.at[slot, rr], send_sem=ssem.at[0],
+            recv_sem=sem(slot, part, half), device_id=(slot, lay), device_id_type=MESH).wait_recv()
+
+    right, left = at(0, 1), at(0, -1)
+    zpeers = [at(dz, 0) for dz in range(1, nz)]
+    for h in range(2):
+        send(0, 0, 0, h, right)
+        send(0, 0, 0, h, left)
+    for zp in zpeers:
+        send(0, 0, 0, None, zp)
+        send(0, 0, 1, None, zp)
+    for h in range(2):
+        send(0, 0, 1, h, right)
+        send(0, 0, 1, h, left)
     gsends = []
     for d in range(1, ns):
         j = lax.rem(s + d, ns)
@@ -122,22 +138,37 @@
             recv_sem=grsem.at[s], device_id=(j, lay), device_id_type=MESH)
         c.start()
         gsends.append(c)
-    for dx in range(1, nx):
-        q = at(0, dx)
-        recv(q, 0)
-        for dz in range(1, nz):
-            send(xo_ref.at[q, parts[0]], q, 0, at(dz, 0))
+    recv(0, -1, 0, 0)
+    send(0, -1, 0, 0, right)
+    recv(0, 1, 0, 1)
+    send(0, 1, 0, 1, left)
+    recv(0, -1, 0, 1)
+    recv(0, 1, 0, 0)
+    for dx in (-1, 1):
+        for zp in zpeers:
+            send(0, dx, 0, None, zp)
+    recv(0, 2, 0, 0)
+    recv(0, 2, 0, 1)
+    for zp in zpeers:
+        send(0, 2, 0, None, zp)
     for dz in range(1, nz):
-        q = at(dz, 0)
-        recv(q, 1)
-        for dx in range(1, nx):
-            send(xo_ref.at[q, parts[1]], q, 1, at(0, dx))
+        recv(dz, 0, 1, None)
+        for h in range(2):
+            send(dz, 0, 1, h, right)
+            send(dz, 0, 1, h, left)
+    for dz in range(nz):
+        recv(dz, -1, 1, 0)
+        send(dz, -1, 1, 0, right)
+        recv(dz, 1, 1, 1)
+        send(dz, 1, 1, 1, left)
     for dz in range(1, nz):
         for dx in range(nx):
-            recv(at(dz, dx), 0)
-    for dx in range(1, nx):
-        for dz in range(nz):
-            recv(at(dz, dx), 1)
+            recv(dz, dx, 0, None)
+    for dz in range(nz):
+        recv(dz, -1, 1, 1)
+        recv(dz, 1, 1, 0)
+        recv(dz, 2, 1, 0)
+        recv(dz, 2, 1, 1)
     for d in range(1, ns):
         i = lax.rem(s + ns - d, ns)
         pltpu.make_async_remote_copy(
@@ -150,12 +181,12 @@
 
 
 def exchange(rotated, outgoing, ns):
-    nx = 4 if ns % 4 == 0 else 1
+    nx = 4
     nz = ns // nx
     t, dim = rotated.shape
     w = outgoing.shape[-1]
-    r1 = (t * 3 // 8) // 16 * 16
-    n_sends = 2 * ((nx - 1) + (nz - 1)) + (nx - 1) * (nz - 1) * 2
+    r1 = t // 8
+    n_sends = 64
     return pl.pallas_call(
         functools.partial(comm_kernel, nx, nz, r1),
         out_shape=(jax.ShapeDtypeStruct((ns, t, dim), rotated.dtype), jax.ShapeDtypeStruct((ns, t, w), outgoing.dtype)),
@@ -163,7 +194,7 @@
         out_specs=(pl.BlockSpec(memory_space=pl.ANY), pl.BlockSpec(memory_space=pl.ANY)),
         scratch_shapes=[
             pltpu.SemaphoreType.DMA((n_sends,)),
-            pltpu.SemaphoreType.DMA((2 * ns,)),
+            pltpu.SemaphoreType.DMA((4 * ns,)),
             pltpu.SemaphoreType.DMA((ns - 1,)),
             pltpu.SemaphoreType.DMA((ns,)),
             pltpu.SemaphoreType.DMA((2,)),

time: 373 us -> 346 us (0.928)
  Pallas kernels: 305 us -> 279 us
    pallas_call x1, Pallas kernels: 273 us -> 221 us  [exchange(): pl.pallas_call(functools.partial(comm_kernel, nx, nz, r1), out_shape=(jax...]
    pallas_call x1, Pallas kernels: 31.9 us -> 57.8 us  [reduce_scores(): pl.pallas_call(functools.partial(reduce_kernel, ns, nl), out_shape=jax.Sh...]
where the time goes in v4:
time: 346 us; the launch traced here: 345 us
  Pallas kernels  279 us (81%)
  matrix products  31.5 us (9%)
  local copies, waits for them, and re-layouts  25.1 us (7%)
  between operations  10.2 us (3%)
    pallas_call x1, Pallas kernels, exchange(): pl.pallas_call(functools.partial(comm_kernel, nx, nz, r1), out_shape=(jax...  221 us
    pallas_call x1, Pallas kernels, reduce_scores(): pl.pallas_call(functools.partial(reduce_kernel, ns, nl), out_shape=jax.Sh...  57.8 us
    unnamed x23, local copies, waits for them, and re-layouts  21 us
    dot_general x1, matrix products, body(): lax.dot_general(gathered.reshape(ns * count, -1), query, (((1,), (1,)), (...  21 us
    dot_general x7, matrix products, body(): jnp.dot(arrived[:, e * rb:(e + 1) * rb], basis_out[0, e], preferred_eleme...  9.67 us

profile of v4, /device:TPU:1, one launch (start us, length us, event | category | flops | bytes accessed | tf_op | source)
XLA Modules:
  0.0 345.3 jit_solution(11962044725360902649)
XLA Ops:
  0.0 1.9 fusion.34
  12.0 1.5 copy.12
  13.5 0.9 convolution_convert_fusion.7
  14.3 1.4 copy.11.x_ref
  15.7 1.8 dynamic-slice_dynamic-update-slice_fusion.15
  17.5 1.7 dynamic-slice_dynamic-update-slice_fusion.14
  19.2 1.6 dynamic-slice_dynamic-update-slice_fusion.13
  20.8 1.6 dynamic-slice_dynamic-update-slice_fusion.12
  22.4 1.7 dynamic-slice_dynamic-update-slice_fusion.11
  24.1 1.7 dynamic-slice_dynamic-update-slice_fusion.10
  25.8 1.7 dynamic-slice_dynamic-update-slice_fusion.9
  27.5 1.6 dynamic-slice_dynamic-update-slice_fusion.8
  29.1 0.7 dynamic-slice_dynamic-update-slice_fusion.7
  34.8 220.7 %shard_map.64 = (bf16[16,128,4096]{2,1,0:T(8,128)(2,1)}, bf16[16,128,896]{2,1,0:T(8,128)(2,1)}) custom-call(bf16[128,4096]{1,0:T(8,128)(2,1)} %copy.11.x_ref, bf16[16,128,896]{2,1,0:T(8,128)(2,1)} %dynamic-slice_dynamic-update-slice_fusion.g_ref), custom_call_target="tpu_custom_call" | custom-call | tf_op jit(solution)/shard_map/pallas_call | solution.py:190
  255.6 1.4 fusion.10
  257.0 1.4 fusion.9
  258.4 1.4 fusion.8
  259.8 1.4 fusion.7
  261.2 1.4 fusion.6
  262.5 1.4 fusion.5
  263.9 1.4 fusion.4
  265.3 21.0 %multiply_reduce_fusion = f32[2048]{0:T(1024)} fusion(bf16[2048,896]{0,1:T(8,128)(2,1)S(1)} %fusion.4, bf16[2048,4096]{1,0:T(8,128)(2,1)} %bitcast.68, bf16[1,896,4096]{2,1,0:T(8,128)(2,1)} %param.8), kind=kOutput, calls=%fused_computation.2 | convolution fusion | flops 15037888512 | bytes 27795456 | tf_op jit(solution)/shard_map/dot_general | solution.py:244
  286.3 57.8 %shard_map.65 = f32[1,128]{1,0:T(1,128)} custom-call(f32[16,1,128]{2,1,0:T(1,128)} %bitcast.66), custom_call_target="tpu_custom_call" | custom-call | tf_op jit(solution)/shard_map/pallas_call | solution.py:209
  344.1 1.2 copy.37
  (13 shorter events, 5.0 us)
Async XLA Ops:
  0.0 13.4 %copy-start = (bf16[1,32,128,128]{3,2,1,0:T(8,128)(2,1)S(1)}, bf16[1,32,128,128]{3,2,1,0:T(8,128)(2,1)}, u32[]{:S(2)}) copy-start(bf16[1,32,128,128]{3,2,1,0:T(8,128)(2,1)} %param.9) | copy-start | bytes 3145732
  15.7 13.4 %copy-start.1 = (bf16[1,128,14336]{2,1,0:T(8,128)(2,1)S(1)}, bf16[1,128,14336]{2,1,0:T(8,128)(2,1)}, u32[]{:S(2)}) copy-start(bf16[1,128,14336]{2,1,0:T(8,128)(2,1)} %param.7) | copy-start | bytes 11010052
  30.6 225.0 %copy-start.2 = (bf16[1,7,128,128]{3,2,1,0:T(8,128)(2,1)S(1)}, bf16[1,7,128,128]{3,2,1,0:T(8,128)(2,1)}, u32[]{:S(2)}) copy-start(bf16[1,7,128,128]{3,2,1,0:T(8,128)(2,1)} %param.10) | copy-start | bytes 688132

commit v5 on v4

--- a/solution.py
+++ b/solution.py
@@ -121,11 +121,12 @@
 
     right, left = at(0, 1), at(0, -1)
     zpeers = [at(dz, 0) for dz in range(1, nz)]
-    for h in range(2):
+    for h in range(2 if r1 else 0):
         send(0, 0, 0, h, right)
         send(0, 0, 0, h, left)
     for zp in zpeers:
-        send(0, 0, 0, None, zp)
+        if r1:
+            send(0, 0, 0, None, zp)
         send(0, 0, 1, None, zp)
     for h in range(2):
         send(0, 0, 1, h, right)
@@ -138,19 +139,20 @@
             recv_sem=grsem.at[s], device_id=(j, lay), device_id_type=MESH)
         c.start()
         gsends.append(c)
-    recv(0, -1, 0, 0)
-    send(0, -1, 0, 0, right)
-    recv(0, 1, 0, 1)
-    send(0, 1, 0, 1, left)
-    recv(0, -1, 0, 1)
-    recv(0, 1, 0, 0)
-    for dx in (-1, 1):
+    if r1:
+        recv(0, -1, 0, 0)
+        send(0, -1, 0, 0, right)
+        recv(0, 1, 0, 1)
+        send(0, 1, 0, 1, left)
+        recv(0, -1, 0, 1)
+        recv(0, 1, 0, 0)
+        for dx in (-1, 1):
+            for zp in zpeers:
+                send(0, dx, 0, None, zp)
+        recv(0, 2, 0, 0)
+        recv(0, 2, 0, 1)
         for zp in zpeers:
-            send(0, dx, 0, None, zp)
-    recv(0, 2, 0, 0)
-    recv(0, 2, 0, 1)
-    for zp in zpeers:
-        send(0, 2, 0, None, zp)
+            send(0, 2, 0, None, zp)
     for dz in range(1, nz):
         recv(dz, 0, 1, None)
         for h in range(2):
@@ -161,7 +163,7 @@
         send(dz, -1, 1, 0, right)
         recv(dz, 1, 1, 1)
         send(dz, 1, 1, 1, left)
-    for dz in range(1, nz):
+    for dz in range(1, nz if r1 else 1):
         for dx in range(nx):
             recv(dz, dx, 0, None)
     for dz in range(nz):
@@ -185,7 +187,7 @@
     nz = ns // nx
     t, dim = rotated.shape
     w = outgoing.shape[-1]
-    r1 = t // 8
+    r1 = 0
     n_sends = 64
     return pl.pallas_call(
         functools.partial(comm_kernel, nx, nz, r1),

time: 346 us -> 360 us (1.040)
  Pallas kernels: 279 us -> 292 us
    pallas_call x1, Pallas kernels: 57.8 us -> 92.5 us  [reduce_scores(): pl.pallas_call(functools.partial(reduce_kernel, ns, nl), out_shape=jax.Sh...]
    pallas_call x1, Pallas kernels: 221 us -> 200 us  [exchange(): pl.pallas_call(functools.partial(comm_kernel, nx, nz, r1), out_shape=(jax...]
where the time goes in v5:
time: 360 us; the launch traced here: 359 us
  Pallas kernels  292 us (81%)
  matrix products  31.5 us (9%)
  local copies, waits for them, and re-layouts  25.1 us (7%)
  between operations  10.2 us (3%)
    pallas_call x1, Pallas kernels, exchange(): pl.pallas_call(functools.partial(comm_kernel, nx, nz, r1), out_shape=(jax...  200 us
    pallas_call x1, Pallas kernels, reduce_scores(): pl.pallas_call(functools.partial(reduce_kernel, ns, nl), out_shape=jax.Sh...  92.5 us
    unnamed x23, local copies, waits for them, and re-layouts  21 us
    dot_general x1, matrix products, body(): lax.dot_general(gathered.reshape(ns * count, -1), query, (((1,), (1,)), (...  21 us
    dot_general x7, matrix products, body(): jnp.dot(arrived[:, e * rb:(e + 1) * rb], basis_out[0, e], preferred_eleme...  9.67 us

profile of v5, /device:TPU:1, one launch (start us, length us, event | category | flops | bytes accessed | tf_op | source)
XLA Modules:
  0.0 359.2 jit_solution(17971484637365721447)
XLA Ops:
  0.0 1.9 fusion.34
  12.0 1.5 copy.12
  13.5 0.9 convolution_convert_fusion.7
  14.3 1.4 copy.11.x_ref
  15.7 1.8 dynamic-slice_dynamic-update-slice_fusion.15
  17.5 1.7 dynamic-slice_dynamic-update-slice_fusion.14
  19.2 1.6 dynamic-slice_dynamic-update-slice_fusion.13
  20.8 1.6 dynamic-slice_dynamic-update-slice_fusion.12
  22.4 1.7 dynamic-slice_dynamic-update-slice_fusion.11
  24.1 1.7 dynamic-slice_dynamic-update-slice_fusion.10
  25.8 1.7 dynamic-slice_dynamic-update-slice_fusion.9
  27.5 1.6 dynamic-slice_dynamic-update-slice_fusion.8
  29.8 0.7 dynamic-slice_dynamic-update-slice_fusion.6
  34.8 200.0 %shard_map.64 = (bf16[16,128,4096]{2,1,0:T(8,128)(2,1)}, bf16[16,128,896]{2,1,0:T(8,128)(2,1)}) custom-call(bf16[128,4096]{1,0:T(8,128)(2,1)} %copy.11.x_ref, bf16[16,128,896]{2,1,0:T(8,128)(2,1)} %dynamic-slice_dynamic-update-slice_fusion.g_ref), custom_call_target="tpu_custom_call" | custom-call | tf_op jit(solution)/shard_map/pallas_call | solution.py:192
  234.8 1.4 fusion.10
  236.2 1.4 fusion.9
  237.6 1.4 fusion.8
  239.0 1.4 fusion.7
  240.4 1.4 fusion.6
  241.8 1.4 fusion.5
  243.2 1.4 fusion.4
  244.6 21.0 %multiply_reduce_fusion = f32[2048]{0:T(1024)} fusion(bf16[2048,896]{0,1:T(8,128)(2,1)S(1)} %fusion.4, bf16[2048,4096]{1,0:T(8,128)(2,1)} %bitcast.68, bf16[1,896,4096]{2,1,0:T(8,128)(2,1)} %param.8), kind=kOutput, calls=%fused_computation.2 | convolution fusion | flops 15037888512 | bytes 27795456 | tf_op jit(solution)/shard_map/dot_general | solution.py:246
  265.6 92.5 %shard_map.65 = f32[1,128]{1,0:T(1,128)} custom-call(f32[16,1,128]{2,1,0:T(1,128)} %bitcast.66), custom_call_target="tpu_custom_call" | custom-call | tf_op jit(solution)/shard_map/pallas_call | solution.py:211
  358.1 1.2 copy.37
  (13 shorter events, 5.0 us)
Async XLA Ops:
  0.0 13.4 %copy-start = (bf16[1,32,128,128]{3,2,1,0:T(8,128)(2,1)S(1)}, bf16[1,32,128,128]{3,2,1,0:T(8,128)(2,1)}, u32[]{:S(2)}) copy-start(bf16[1,32,128,128]{3,2,1,0:T(8,128)(2,1)} %param.9) | copy-start | bytes 3145732
  15.7 13.4 %copy-start.1 = (bf16[1,128,14336]{2,1,0:T(8,128)(2,1)S(1)}, bf16[1,128,14336]{2,1,0:T(8,128)(2,1)}, u32[]{:S(2)}) copy-start(bf16[1,128,14336]{2,1,0:T(8,128)(2,1)} %param.7) | copy-start | bytes 11010052
  30.6 204.3 %copy-start.2 = (bf16[1,7,128,128]{3,2,1,0:T(8,128)(2,1)S(1)}, bf16[1,7,128,128]{3,2,1,0:T(8,128)(2,1)}, u32[]{:S(2)}) copy-start(bf16[1,7,128,128]{3,2,1,0:T(8,128)(2,1)} %param.10) | copy-start | bytes 688132
